TPU v7x, 32 devices: a whole 2x2x4 slice. The times are simulated.
32 devices in a mesh: grp: 4 (over y, x), dev: 8 (over z, core).
Axes of the slice: x: 2, y: 2, z: 4, core: 2. Of those that a mesh axis runs over, the one named last changes fastest.
Arguments:
- features: bfloat16 [4096, 768], P(('grp', 'dev')), may hold values from -6 to 6
- neighbours: int32 [4096, 25], P(('grp', 'dev')), may hold values from 0 to 4095, as said below
- neighbour_mask: int32 [4096, 25], P(('grp', 'dev')), may hold values from 0 to 1, as said below
- layer2_position: int32 [4096], P(('grp', 'dev')), may hold values from 0 to 4095, as said below
- self_weight1: bfloat16 [768, 1024], replicated, may hold values from -0.21875 to 0.21875
- neigh_weight1: bfloat16 [768, 1024], replicated, may hold values from -0.4375 to 0.4375
- self_weight2: bfloat16 [1024, 1024], replicated, may hold values from -0.1875 to 0.1875
- neigh_weight2: bfloat16 [1024, 1024], replicated, may hold values from -0.375 to 0.375
Outputs:
- embeddings: bfloat16 [4096, 1024], P(('grp', 'dev'))
Inputs may be any that keep to these rules, and one draw needn't show every extreme that they name: `neighbours`: node n is owned by device n // 128 (devices numbered grp-major). Slot 0 of every node is valid. Of one device's nodes, at most 6 valid slots name nodes of any one other device, and exactly 6 do for some other device; 93 slots of one device name other devices' nodes, all of them valid. Invalid slots hold ids of the device's own nodes. `neighbour_mask`: values 0 or 1; 1 at slot 0 and wherever the neighbour lies on another device. A permutation of the nodes; a node's new owner, layer2_position // 128, is in the same group as its old one. One device hands exactly 32 nodes to each owner of its group whose index within the group differs from its own by an even number, and none to the others.
All inputs are finite; a program needn't handle non-finite values.
Results may differ from a plain program's by a relative error of at most 0.0052.
Values may be sent and summed in bfloat16 or wider, within the bound.
No kernel may reach another device: no remote copies, remote signals or barrier semaphores. Data moves between devices by JAX's collectives and lax.ppermute only.
A program may use at most 64 MiB of HBM per device.

v0:
```python
import functools

import jax
import jax.numpy as jnp
from jax import lax
from jax.experimental import pallas as pl
from jax.experimental.pallas import tpu as pltpu
from jax.sharding import PartitionSpec as P


CAP = 6
BOTH = ("grp", "dev")
F32 = jnp.float32
BF16 = jnp.bfloat16
I32 = jnp.int32


def divide(values, by):
    if by & (by - 1) == 0:
        return values >> (by.bit_length() - 1)
    return (values * (-(-(1 << 16) // by))) >> 16


def iota(shape, dim):
    return lax.broadcasted_iota(I32, shape, dim)


def bits(condition):
    return jnp.where(condition, 1.0, 0.0)


def earlier(count):
    return bits(iota((count, count), 0) < iota((count, count), 1)).astype(BF16)


def dot(left, right):
    return jnp.dot(left, right, preferred_element_type=F32)


def dot_lanes(left, right):
    return lax.dot_general(left, right, (((1,), (1,)), ((), ())), preferred_element_type=F32)


def near_by(n):
    return [pl.BlockSpec(memory_space=pltpu.VMEM)] * n


def far_off(n):
    return [pl.BlockSpec(memory_space=pltpu.HBM)] * n


def call(kernel, outs, remote, operands, scratch, flops, limit=24 << 20, away=0):
    single = not isinstance(outs, tuple)
    leaves = (outs,) if single else outs
    moved = sum(a.size * a.dtype.itemsize for a in (*remote, *operands, *leaves))
    return pl.pallas_call(
        kernel,
        out_shape=outs if single else (*(pltpu.HBM(a.shape, a.dtype) for a in leaves[:away]), *leaves[away:]),
        in_specs=far_off(len(remote)) + near_by(len(operands)),
        out_specs=near_by(1)[0] if single else far_off(away) + near_by(len(leaves) - away),
        scratch_shapes=scratch,
        compiler_params=pltpu.CompilerParams(vmem_limit_bytes=limit),
        cost_estimate=pl.CostEstimate(flops=flops, bytes_accessed=moved, transcendentals=0),
    )(*(pltpu.with_memory_space_constraint(a, pltpu.HBM) for a in remote), *operands)


def fetches(weight_ref, held, sems):
    pieces = sems.shape[0]
    depth = weight_ref.shape[0] // pieces
    return [
        pltpu.make_async_copy(
            weight_ref.at[pl.ds(i * depth, depth)], held.at[pl.ds(i * depth, depth)], sems.at[i]
        )
        for i in range(pieces)
    ]


def dot_fetched(left, held, copies):
    depth = held.shape[0] // len(copies)
    result = None
    for i, copy in enumerate(copies):
        copy.wait()
        part = dot(left[:, i * depth : (i + 1) * depth], held[i * depth : (i + 1) * depth])
        result = part if result is None else result + part
    return result


def seat():
    member = lax.axis_index("dev")
    return lax.axis_index("grp"), member >> 1, member & 1


def wrap(value, size):
    value = jnp.where(value < 0, value + size, value)
    return jnp.where(value >= size, value - size, value)


def device_at(index, groups, members):
    group, height, core = seat()
    step = divide(index, 2 * groups)
    mate = index - step * 2 * groups
    height = wrap(height + step, members // 2)
    return ((mate >> 1) ^ group) * members + 2 * height + ((mate & 1) ^ core), group * members + 2 * height + core


def apart(device, members):
    group, height, core = seat()
    its_group = divide(device, members)
    member = device - its_group * members
    return wrap((member >> 1) - height, members // 2), its_group ^ group, (member & 1) ^ core


def ask_kernel(groups, members, ids_hbm, mask_hbm, pos_hbm, key_ref, local_ref, span_ref, *refs):
    ask_refs, (ids, mask, pos_ref, sems) = refs[:-4], refs[-4:]
    peers = groups * members
    degree, rows = ids.shape
    copies = [
        pltpu.make_async_copy(ids_hbm, ids, sems.at[0]),
        pltpu.make_async_copy(mask_hbm, mask, sems.at[1]),
        pltpu.make_async_copy(pos_hbm, pos_ref, sems.at[2]),
    ]
    for copy in copies:
        copy.start()
    own = lax.axis_index("grp") * members + lax.axis_index("dev")
    peer, new_home = device_at(iota((peers, rows), 0), groups, members)
    prefix = earlier(rows)
    for copy in copies:
        copy.wait()
    slots = jnp.where(mask[...] > 0, ids[...], -1)
    owner = divide(jnp.maximum(slots, 0), rows)
    row = slots - owner * rows
    live = slots >= 0
    here = owner == own
    key = jnp.where(live & jnp.logical_not(here), owner, -1)
    half = CAP // 2
    width = (rows - 1).bit_length()
    top = width * (half - 1)
    low = jnp.zeros((peers, rows), I32)
    high = jnp.zeros((peers, rows), I32)
    total = jnp.zeros((peers, rows), I32)
    for s in range(degree):
        hit = key[s : s + 1] == peer
        high = jnp.where(hit, (high << width) | (low >> top), high)
        low = jnp.where(hit, ((low & ((1 << top) - 1)) << width) | row[s : s + 1], low)
        total += jnp.where(hit, 1, 0)
    before = dot(total.astype(F32).astype(BF16), prefix).astype(I32)
    packed = [jnp.where(before == 0, low, 0), jnp.where(before == 0, high, jnp.where(before == half, low, 0))]
    for k in range(1, half):
        shift, rest = width * k, width * (half - k)
        inside = before == k
        packed[0] = jnp.where(inside, (low & ((1 << rest) - 1)) << shift, packed[0])
        packed[1] = jnp.where(inside, (high << shift) | (low >> rest), packed[1])
        packed[1] = jnp.where(before == half + k, low << shift, packed[1])
    lane = iota((peers, rows), 1)
    wanted = jnp.zeros((peers, rows), I32)
    for w, word in enumerate(packed):
        word = jnp.broadcast_to(jnp.sum(word.astype(F32), axis=1, keepdims=True).astype(I32), (peers, rows))
        for k in range(half):
            wanted = jnp.where(lane == w * half + k, (word >> (width * k)) & ((1 << width) - 1), wanted)
    pos = pos_ref[...]
    place = jnp.where(divide(pos, rows) == new_home, pos - divide(pos, rows) * rows + 1, 0)
    asks = place + wanted * (2 * rows)
    for q, ref in enumerate(ask_refs):
        ref[...] = asks[q * 2 * groups : (q + 1) * 2 * groups]
    key_ref[...] = key
    local_ref[...] = jnp.where(live & here, row, -1)
    span_ref[0] = before
    span_ref[1] = total


def plan_kernel(
    peers, degree, features_hbm, key_ref, local_ref, span_ref, near_ref, far_ref, order_ref, features_ref, sems
):
    taken = pltpu.make_async_copy(features_hbm, features_ref, sems.at[0])
    taken.start()
    rows = features_ref.shape[0]
    local = local_ref[...]
    node = iota((rows, rows), 0)
    near = jnp.zeros((rows, rows), F32)
    for s in range(degree):
        near += bits(local[s : s + 1] == node)
    near = near.T.astype(BF16)
    near_ref[...] = near
    before, total = span_ref[0], span_ref[1]
    far = [bits((before <= k) & (k < before + total)).astype(BF16) for k in range(CAP)]
    far = jnp.concatenate(far, axis=0)
    size = peers * CAP
    line = iota((size, size), 0)
    peer = divide(line, CAP)
    order = bits(iota((size, size), 1) == (line - peer * CAP) * peers + peer).astype(BF16)
    order_ref[...] = order
    far_ref[:, :size] = dot(order, far).T.astype(BF16)
    live = bits((local >= 0) | (key_ref[...] >= 0))
    count = jnp.broadcast_to(jnp.sum(live, axis=0, keepdims=True), (rows, rows)).T.astype(BF16)
    far_ref[:, size:] = count[:, : far_ref.shape[1] - size]
    taken.wait()


def store_rows(reply_ref, rows):
    peers, pairs, two, width = reply_ref.shape
    reply_ref[...] = rows.reshape(peers, pairs, two, width)


def load_rows(answer_ref):
    peers, pairs, two, width = answer_ref.shape
    return answer_ref[...].reshape(peers * pairs * two, width)


def picks_of(wanted, order):
    lane = iota(wanted.shape, 1)
    picks = [bits(wanted[:, k : k + 1] == lane).astype(BF16) for k in range(CAP)]
    return dot(order, jnp.concatenate(picks, axis=0)).astype(BF16)


def sort_kernel(groups, *refs):
    steps = len(refs) - groups
    asked = jnp.concatenate([ref[...] for ref in refs[:steps]], axis=0)
    peers, rows = asked.shape
    wanted = divide(asked, 2 * rows)
    line = iota((peers, peers), 0)
    mate = divide(line, steps)
    pick = bits(iota((peers, peers), 1) == (line - mate * steps) * 2 * groups + mate).astype(BF16)
    sorted_rows = dot(pick, wanted.astype(F32).astype(BF16)).astype(I32)
    for m, ref in enumerate(refs[steps:]):
        ref[...] = sorted_rows[m * 2 * steps : (m + 1) * 2 * steps]


def serve_kernel(groups, steps, order_ref, *refs):
    asked_refs, refs = refs[:steps], refs[steps:]
    table_refs, reply_refs = refs[: 2 * groups], refs[2 * groups :]
    asked = jnp.concatenate([ref[...] for ref in asked_refs], axis=0)
    pick = picks_of(divide(asked, 2 * asked.shape[1]), order_ref[...])
    line = divide(iota(pick.shape, 0), CAP)
    mate = line - divide(line, 2 * groups) * 2 * groups
    rows = None
    for m in range(groups):
        left = [jnp.where(mate == 2 * m + side, pick, jnp.zeros_like(pick)) for side in range(2)]
        table = jnp.concatenate([table_refs[2 * m][...], table_refs[2 * m + 1][...]], axis=0)
        part = dot(jnp.concatenate(left, axis=1), table)
        rows = part if rows is None else rows + part
    rows = rows.astype(BF16)
    block = rows.shape[0] // steps
    for q, ref in enumerate(reply_refs):
        ref[...] = rows[q * block : (q + 1) * block]


def pick_kernel(members, kept_ref, passed_ref, pick_ref):
    kept = kept_ref[...]
    peers = kept.shape[0]
    steps = members // 2
    half = divide(iota(kept.shape, 0), steps)
    wanted = jnp.where((half & 1) == 0, kept, passed_ref[...])
    size = peers * CAP
    line = iota((size, size), 0)
    device = divide(line, CAP)
    step, group, core = apart(device, members)
    row = (2 * group + core) * steps + wrap(-step, steps)
    order = bits(iota((size, size), 1) == (line - device * CAP) * peers + row).astype(BF16)
    pick_ref[...] = picks_of(wanted, order)


def over_count(summed, far):
    size = far.shape[1] - 8
    return (summed / far[:, size : size + 1].astype(F32)).astype(BF16)


def layer_one_kernel(features_ref, near_ref, far_ref, pick_ref, *refs):
    answer_refs, (answer_hbm, mean_hbm, reply_ref, kept, mean_ref, sems) = refs[:-6], refs[-6:]
    answer = jnp.concatenate([ref[...] for ref in answer_refs], axis=0)
    kept[...] = answer
    saves = [
        pltpu.make_async_copy(kept, answer_hbm, sems.at[0]),
        pltpu.make_async_copy(mean_ref, mean_hbm, sems.at[1]),
    ]
    saves[0].start()
    far = far_ref[...]
    mean = over_count(dot(near_ref[...], features_ref[...]) + dot(far[:, : answer.shape[0]], answer), far)
    mean_ref[...] = mean
    saves[1].start()
    store_rows(reply_ref, dot(pick_ref[...], mean).astype(BF16))
    for save in saves:
        save.wait()


def between_kernel(
    groups, members, self_one_hbm, neigh_one_hbm, self_two_hbm, neigh_two_hbm, pos_hbm, features_hbm, answer_hbm, mean_hbm,
    near_ref, far_ref, *refs,
):
    asked_refs, refs = refs[: members // 2], refs[members // 2 :]
    between_body(
        groups, members, self_one_hbm, neigh_one_hbm, self_two_hbm, neigh_two_hbm, pos_hbm, features_hbm, answer_hbm, mean_hbm,
        near_ref, far_ref, asked_refs, *refs,
    )


def between_body(
    groups, members, self_one_hbm, neigh_one_hbm, self_two_hbm, neigh_two_hbm, pos_hbm, features_hbm, answer_hbm, mean_hbm,
    near_ref, far_ref, asked_refs,
    final_hbm, place_hbm, base_ref, far_moved_ref, neigh_one_ref, ready_ref,
    held_one, held_two, rest, features_ref, answer_ref, mean_ref, final_ref, place_ref, pos_ref, sems,
):
    ready = ready_ref.shape[0]
    copies = [
        pltpu.make_async_copy(pos_hbm, pos_ref, sems.at[0]),
        pltpu.make_async_copy(self_one_hbm, held_one, sems.at[1]),
        pltpu.make_async_copy(neigh_one_hbm, neigh_one_ref, sems.at[2]),
        pltpu.make_async_copy(self_two_hbm, held_two, sems.at[3]),
        pltpu.make_async_copy(neigh_two_hbm.at[pl.ds(0, ready)], ready_ref, sems.at[4]),
        pltpu.make_async_copy(neigh_two_hbm.at[pl.ds(ready, rest.shape[0])], rest, sems.at[5]),
    ]
    inputs = [
        pltpu.make_async_copy(features_hbm, features_ref, sems.at[6]),
        pltpu.make_async_copy(answer_hbm, answer_ref, sems.at[7]),
        pltpu.make_async_copy(mean_hbm, mean_ref, sems.at[8]),
    ]
    for copy in (*inputs, *copies):
        copy.start()
    rows = features_ref.shape[0]
    capacity = 2 * rows // members
    me = lax.axis_index("dev")
    first = lax.axis_index("grp") * members
    line = iota((rows, rows), 0)
    step = divide(line, capacity)
    rank = line - step * capacity
    target = me + 2 * step
    target = jnp.where(target >= members, target - members, target)
    prefix = earlier(rows)
    copies[0].wait()
    goes = target == divide(pos_ref[...], rows) - first
    before = dot(bits(goes).astype(BF16), prefix).astype(I32)
    move = bits(goes & (before == rank)).astype(BF16)
    near = dot(move, near_ref[...]).astype(BF16)
    size = base_ref.shape[0]
    slot = iota((size, size), 0)
    device = divide(slot, CAP)
    up, group, core = apart(device, members)
    came = ((up * groups + group) * 2 + core) * CAP + slot - device * CAP
    resort = bits(iota((size, size), 1) == came).astype(BF16)
    far = dot(move, far_ref[...]).astype(BF16)
    far_moved_ref[:, size:] = far[:, size:]
    far_moved_ref[:, :size] = dot_lanes(far[:, :size], resort).astype(BF16)
    place = jnp.zeros((rows, rows), F32)
    for q in range(members // 2):
        sent = asked_refs[q][0:1] & (2 * rows - 1)
        valid = jnp.broadcast_to(sent > 0, (rows, rows))
        before = dot(bits(valid).astype(BF16), prefix).astype(I32)
        lands = bits(sent - 1 == line).astype(BF16)
        comes = bits(valid & (step == q) & (before == rank)).astype(BF16)
        place += dot_lanes(lands, comes)
    place_ref[...] = place.astype(BF16)
    placed = pltpu.make_async_copy(place_ref, place_hbm, sems.at[9])
    placed.start()
    for copy in (*inputs, copies[1]):
        copy.wait()
    own = dot(features_ref[...], held_one[...])
    base_ref[...] = dot(dot(resort, answer_ref[...]).astype(BF16), held_one[...]).astype(BF16)
    copies[2].wait()
    hidden = jnp.maximum(own + dot(mean_ref[...], neigh_one_ref[...]), 0.0).astype(BF16)
    mean = over_count(dot(near, hidden), far)
    moved = dot(move, hidden).astype(BF16)
    copies[3].wait()
    final = dot(moved, held_two[...])
    copies[4].wait()
    final += dot(mean[:, :ready], ready_ref[...])
    copies[5].wait()
    final_ref[...] = final + dot(mean[:, ready:], rest[...])
    away = pltpu.make_async_copy(final_ref, final_hbm, sems.at[10])
    away.start()
    away.wait()
    placed.wait()


def layer_two_kernel(neigh_two_hbm, final_hbm, neigh_one_ref, ready_ref, base_ref, answer_ref, far_ref, *refs):
    outs, held, final_ref, sems = refs[:-3], refs[-3], refs[-2], refs[-1]
    ready = ready_ref.shape[0]
    pieces = sems.shape[0] - 1
    copies = fetches(neigh_two_hbm.at[pl.ds(ready, held.shape[0])], held, sems.at[pl.ds(0, pieces)])
    last = pltpu.make_async_copy(final_hbm, final_ref, sems.at[pieces])
    for copy in (*copies, last):
        copy.start()
    far = far_ref[...]
    other = jnp.maximum(base_ref[...].astype(F32) + dot(load_rows(answer_ref), neigh_one_ref[...]), 0.0).astype(BF16)
    mean = over_count(dot(far[:, : other.shape[0]], other), far)
    final = dot(mean[:, :ready], ready_ref[...]) + dot_fetched(mean[:, ready:], held, copies)
    last.wait()
    final = (final + final_ref[...]).astype(BF16)
    capacity = outs[0].shape[0]
    for q, ref in enumerate(outs):
        ref[...] = final[q * capacity : (q + 1) * capacity]


def scatter_kernel(place_ref, *refs):
    out_ref = refs[-1]
    arrived = jnp.concatenate([ref[...] for ref in refs[:-1]], axis=0)
    out_ref[...] = dot(place_ref[...], arrived).astype(BF16)


def compute(features, neighbours, neighbour_mask, layer2_position, self_weight1, neigh_weight1, self_weight2, neigh_weight2):
    rows, degree = neighbours.shape
    members = lax.axis_size("dev")
    peers = lax.axis_size("grp") * members
    width_in, width = self_weight1.shape
    steps = members // 2
    capacity = rows // steps
    size = peers * CAP
    early = width // 2
    shape = jax.ShapeDtypeStruct
    copies = pltpu.SemaphoreType.DMA

    pos = layer2_position.reshape(1, rows)
    groups = peers // members
    mates = 2 * groups

    def shifts(by):
        return [(i, (i + by) % members) for i in range(members)]

    def across(by):
        return [(i, i ^ by) for i in range(groups)]

    pairs = [(i, i ^ 1) for i in range(members)]
    tables = [features] + [lax.ppermute(features, "grp", across(m)) for m in range(1, groups)]
    others = [lax.ppermute(t, "dev", pairs) for t in tables]
    key, local, span, *asks = call(
        functools.partial(ask_kernel, groups, members),
        (
            shape((degree, rows), I32),
            shape((degree, rows), I32),
            shape((2, peers, rows), I32),
            *(shape((mates, rows), I32) for _ in range(steps)),
        ),
        (neighbours.T, neighbour_mask.T, pos),
        (),
        [pltpu.VMEM((degree, rows), I32), pltpu.VMEM((degree, rows), I32), pltpu.VMEM((1, rows), I32), copies((3,))],
        2 * peers * rows * rows,
    )
    asked = [asks[0]] + [lax.ppermute(asks[q], "dev", shifts(2 * q)) for q in range(1, steps)]
    near, far, order, table = call(
        functools.partial(plan_kernel, peers, degree),
        (
            shape((rows, rows), BF16),
            shape((rows, size + 8), BF16),
            shape((size, size), BF16),
            shape((rows, width_in), BF16),
        ),
        (features,),
        (key, local, span),
        [copies((1,))],
        2 * size * size * rows,
        limit=40 << 20,
    )
    by_mate = call(
        functools.partial(sort_kernel, groups),
        tuple(shape((2 * steps, rows), I32) for _ in range(groups)),
        (),
        asked,
        [],
        2 * peers * peers * rows,
    )
    kept_asks = jnp.concatenate([by_mate[0]] + [lax.ppermute(by_mate[m], "grp", across(m)) for m in range(1, groups)])
    passed_asks = lax.ppermute(kept_asks, "dev", pairs)
    replies = call(
        functools.partial(serve_kernel, groups, steps),
        tuple(shape((mates * CAP, width_in), BF16) for _ in range(steps)),
        (),
        (order, *asked, *(t for pair in zip([table, *tables[1:]], others) for t in pair)),
        [],
        2 * size * rows * mates * width_in,
    )
    answers = [replies[0]] + [lax.ppermute(replies[q], "dev", shifts(-2 * q)) for q in range(1, steps)]
    pick = call(
        functools.partial(pick_kernel, members),
        shape((size, rows), BF16),
        (),
        (kept_asks, passed_asks),
        [],
        2 * size * size * rows,
    )
    kept, mean, reply_two = call(
        layer_one_kernel,
        (
            shape((size, width_in), BF16),
            shape((rows, width_in), BF16),
            shape((peers, CAP // 2, 2, width_in), BF16),
        ),
        (),
        (table, near, far, pick, *answers),
        [pltpu.VMEM((size, width_in), BF16), pltpu.VMEM((rows, width_in), BF16), copies((2,))],
        2 * rows * width_in * (size + rows) + 2 * size * rows * width_in,
        away=2,
    )
    answer_two = lax.all_to_all(reply_two, BOTH, 0, 0, tiled=True)
    final, place, base, far_moved, weight, ready = call(
        functools.partial(between_kernel, groups, members),
        (
            shape((rows, width), F32),
            shape((rows, rows), BF16),
            shape((size, width), BF16),
            shape((rows, size + 8), BF16),
            shape((width_in, width), BF16),
            shape((early, width), BF16),
        ),
        (self_weight1, neigh_weight1, self_weight2, neigh_weight2, pos, features, kept, mean),
        (near, far, *asked),
        [
            pltpu.VMEM((width_in, width), BF16),
            pltpu.VMEM((width, width), BF16),
            pltpu.VMEM((width - early, width), BF16),
            pltpu.VMEM((rows, width_in), BF16),
            pltpu.VMEM((size, width_in), BF16),
            pltpu.VMEM((rows, width_in), BF16),
            pltpu.VMEM((rows, width), F32),
            pltpu.VMEM((rows, rows), BF16),
            pltpu.VMEM((1, rows), I32),
            copies((11,)),
        ],
        2 * width * (rows * (2 * width_in + rows + 2 * width) + size * width_in),
        limit=48 << 20,
        away=2,
    )
    finals = call(
        layer_two_kernel,
        tuple(shape((capacity, width), BF16) for _ in range(steps)),
        (neigh_weight2, final),
        (weight, ready, base, answer_two, far_moved),
        [pltpu.VMEM((width - early, width), BF16), pltpu.VMEM((rows, width), F32), copies((3,))],
        2 * width * (size * width_in + rows * (size + width)),
        limit=48 << 20,
    )
    arrived = [finals[0]]
    for q in range(1, steps):
        arrived.append(lax.ppermute(finals[q], "dev", shifts(2 * q)))
    return call(scatter_kernel, shape((rows, width), BF16), (), (place, *arrived), [], 2 * rows * rows * width)


def solution(mesh):
    return jax.shard_map(
        compute,
        mesh=mesh,
        in_specs=(
            P(BOTH, None),
            P(BOTH, None),
            P(BOTH, None),
            P(BOTH),
            P(),
            P(),
            P(),
            P(),
        ),
        out_specs=P(BOTH, None),
        check_vma=False,
    )
```

profile of v0, /device:TPU:0, one launch (start us, length us, event | category | flops | bytes accessed | tf_op | source)
XLA Modules:
  0.0 63.0 jit_solution(9378077465261359343)
XLA Ops:
  0.0 3.0 %collective-permute-start.10 = (bf16[128,768]{1,0:T(8,128)(2,1)}, bf16[128,768]{1,0:T(8,128)(2,1)S(1)}, u32[]{:S(2)}, u32[]{:S(2)}) collective-permute-start(bf16[128,768]{1,0:T(8,128)(2,1)} %features_hbm.3), channel_id=1, source_target_pairs={{0,16},{8,24},{16,0},{24,8},{1,17},{9,25},{17,1},{25,9},{2,18},{10... | collective-permute-start | bytes 589832 | tf_op jit(solution)/shard_map/ppermute | solution.py:421
  3.0 1.5 %collective-permute-start.8 = (bf16[128,768]{1,0:T(8,128)(2,1)}, bf16[128,768]{1,0:T(8,128)(2,1)S(1)}, u32[]{:S(2)}, u32[]{:S(2)}) collective-permute-start(bf16[128,768]{1,0:T(8,128)(2,1)} %features_hbm.3), channel_id=1, source_target_pairs={{0,8},{8,0},{16,24},{24,16},{1,9},{9,1},{17,25},{25,17},{2,10},{10... | collective-permute-start | bytes 589832 | tf_op jit(solution)/shard_map/ppermute | solution.py:421
  4.5 0.0 collective-permute-start.12
  4.5 1.1 %shard_map.82 = (s32[25,128]{1,0:T(8,128)S(1)}, s32[25,128]{1,0:T(8,128)S(1)}, s32[2,32,128]{2,1,0:T(8,128)S(1)}, s32[8,128]{1,0:T(8,128)S(1)}, s32[8,128]{1,0:T...) custom-call(s32[25,128]{1,0:T(8,128)} %bitcast.3, s32[25,128]{1,0:T(8,128)} %bitcast.4, s32[1,128]{1,0:T(1,128)} %bitcast.5), custom_call_target="tpu_custom_call" | custom-call | flops 1048576 | bytes 100864 | tf_op jit(solution)/shard_map/pallas_call | solution.py:56
  5.6 2.1 %collective-permute-start = (s32[8,128]{1,0:T(8,128)S(1)}, s32[8,128]{1,0:T(8,128)S(1)}, u32[]{:S(2)}, u32[]{:S(2)}) collective-permute-start(s32[8,128]{1,0:T(8,128)S(1)} %get-tuple-element.44), channel_id=1, source_target_pairs={{0,2},{1,3},{2,4},{3,5},{4,6},{5,7},{6,0},{7,1},{8,10},{9,11},{10,... | collective-permute-start | bytes 12296 | tf_op jit(solution)/shard_map/ppermute | solution.py:436
  7.7 2.6 %collective-permute-start.1 = (s32[8,128]{1,0:T(8,128)S(1)}, s32[8,128]{1,0:T(8,128)S(1)}, u32[]{:S(2)}, u32[]{:S(2)}) collective-permute-start(s32[8,128]{1,0:T(8,128)S(1)} %get-tuple-element.45), channel_id=1, source_target_pairs={{0,4},{1,5},{2,6},{3,7},{4,0},{5,1},{6,2},{7,3},{8,12},{9,13},{10,... | collective-permute-start | bytes 12296 | tf_op jit(solution)/shard_map/ppermute | solution.py:436
  10.3 1.0 %collective-permute-done.refs_1_ = s32[8,128]{1,0:T(8,128)S(1)} collective-permute-done((s32[8,128]{1,0:T(8,128)S(1)}, s32[8,128]{1,0:T(8,128)S(1)}, u32[]{:S(2)}, u32[]{:S(2)}) %collective-permute-start) | collective-permute-done | bytes 4128 | tf_op jit(solution)/shard_map/ppermute | solution.py:436
  11.3 2.0 %collective-permute-start.2 = (s32[8,128]{1,0:T(8,128)S(1)}, s32[8,128]{1,0:T(8,128)S(1)}, u32[]{:S(2)}, u32[]{:S(2)}) collective-permute-start(s32[8,128]{1,0:T(8,128)S(1)} %get-tuple-element.46), channel_id=1, source_target_pairs={{0,6},{1,7},{2,0},{3,1},{4,2},{5,3},{6,4},{7,5},{8,14},{9,15},{10,... | collective-permute-start | bytes 12296 | tf_op jit(solution)/shard_map/ppermute | solution.py:436
  13.3 1.0 %shard_map.83 = (bf16[128,128]{1,0:T(8,128)(2,1)S(1)}, bf16[128,200]{1,0:T(8,128)(2,1)S(1)}, bf16[192,192]{1,0:T(8,128)(2,1)S(1)}, bf16[128,768]{1,0:T(8,128)(2,1)S(1)}) custom-call(bf16[128,768]{1,0:T(8,128)(2,1)} %features_hbm.3, s32[25,128]{1,0:T(8,128)S(1)} %get-tuple-element.37.key_ref, s32[25,128]{1,0:T(8,128)S(1)} %get-tuple-element.38.local_ref, ...), custom_call_target="tpu_custom_call" | custom-call | flops 9437184 | bytes 609280 | tf_op jit(solution)/shard_map/pallas_call | solution.py:56
  14.3 0.0 collective-permute-done.1.refs_2_
  14.4 0.1 collective-permute-start.7
  14.4 0.5 collective-permute-done.2.refs_3_
  14.9 0.1 shard_map.84
  15.1 1.7 %collective-permute-start.3 = (s32[8,128]{1,0:T(8,128)S(1)}, s32[8,128]{1,0:T(8,128)S(1)}, u32[]{:S(2)}, u32[]{:S(2)}) collective-permute-start(s32[8,128]{1,0:T(8,128)S(1)} %get-tuple-element.48), channel_id=1, source_target_pairs={{0,8},{8,0},{16,24},{24,16},{1,9},{9,1},{17,25},{25,17},{2,10},{10... | collective-permute-start | bytes 12296 | tf_op jit(solution)/shard_map/ppermute | solution.py:459
  16.8 1.9 %collective-permute-done.3 = s32[8,128]{1,0:T(8,128)S(1)} collective-permute-done((s32[8,128]{1,0:T(8,128)S(1)}, s32[8,128]{1,0:T(8,128)S(1)}, u32[]{:S(2)}, u32[]{:S(2)}) %collective-permute-start.3) | collective-permute-done | bytes 4128 | tf_op jit(solution)/shard_map/ppermute | solution.py:459
  18.7 1.8 %collective-permute-start.4 = (s32[8,128]{1,0:T(8,128)S(1)}, s32[8,128]{1,0:T(8,128)S(1)}, u32[]{:S(2)}, u32[]{:S(2)}) collective-permute-start(s32[8,128]{1,0:T(8,128)S(1)} %get-tuple-element.49), channel_id=1, source_target_pairs={{0,16},{8,24},{16,0},{24,8},{1,17},{9,25},{17,1},{25,9},{2,18},{10... | collective-permute-start | bytes 12296 | tf_op jit(solution)/shard_map/ppermute | solution.py:459
  20.4 0.0 collective-permute-done.10.refs_8_
  20.4 0.0 collective-permute-start.11
  20.4 0.0 collective-permute-done.8.refs_6_
  20.4 0.5 collective-permute-start.9
  21.0 0.0 collective-permute-done.12.refs_10_
  21.0 0.1 collective-permute-start.13
  21.0 1.2 %collective-permute-done.4 = s32[8,128]{1,0:T(8,128)S(1)} collective-permute-done((s32[8,128]{1,0:T(8,128)S(1)}, s32[8,128]{1,0:T(8,128)S(1)}, u32[]{:S(2)}, u32[]{:S(2)}) %collective-permute-start.4) | collective-permute-done | bytes 4128 | tf_op jit(solution)/shard_map/ppermute | solution.py:459
  22.3 2.7 %collective-permute-start.5 = (s32[8,128]{1,0:T(8,128)S(1)}, s32[8,128]{1,0:T(8,128)S(1)}, u32[]{:S(2)}, u32[]{:S(2)}) collective-permute-start(s32[8,128]{1,0:T(8,128)S(1)} %get-tuple-element.50), channel_id=1, source_target_pairs={{0,24},{8,16},{16,8},{24,0},{1,25},{9,17},{17,9},{25,1},{2,26},{10... | collective-permute-start | bytes 12296 | tf_op jit(solution)/shard_map/ppermute | solution.py:459
  25.0 0.0 collective-permute-done.7.refs_5_
  25.0 0.0 collective-permute-done.11.refs_9_
  25.0 0.0 collective-permute-done.9.refs_7_
  25.0 0.0 collective-permute-done.13.refs_11_
  25.0 0.7 %shard_map.86 = (bf16[48,768]{1,0:T(8,128)(2,1)S(1)}, bf16[48,768]{1,0:T(8,128)(2,1)S(1)}, bf16[48,768]{1,0:T(8,128)(2,1)S(1)}, bf16[48,768]{1,0:T(8,128)(2,1)S(1)}) custom-call(bf16[192,192]{1,0:T(8,128)(2,1)S(1)} %get-tuple-element.51.order_ref, s32[8,128]{1,0:T(8,128)S(1)} %get-tuple-element.43.refs_0_, s32[8,128]{1,0:T(8,128)S(1)} %collective-permute-done.refs_1_, ...), custom_call_target="tpu_custom_call" | custom-call | flops 301989888 | bytes 1957888 | tf_op jit(solution)/shard_map/pallas_call | solution.py:56
  25.7 3.6 %collective-permute-start.14 = (bf16[48,768]{1,0:T(8,128)(2,1)S(1)}, bf16[48,768]{1,0:T(8,128)(2,1)S(1)}, u32[]{:S(2)}, u32[]{:S(2)}) collective-permute-start(bf16[48,768]{1,0:T(8,128)(2,1)S(1)} %get-tuple-element.53), channel_id=1, source_target_pairs={{0,6},{1,7},{2,0},{3,1},{4,2},{5,3},{6,4},{7,5},{8,14},{9,15},{10,... | collective-permute-start | bytes 221192 | tf_op jit(solution)/shard_map/ppermute | solution.py:469
  29.3 0.0 collective-permute-start.15
  29.3 0.6 %collective-permute-start.16 = (bf16[48,768]{1,0:T(8,128)(2,1)S(1)}, bf16[48,768]{1,0:T(8,128)(2,1)S(1)}, u32[]{:S(2)}, u32[]{:S(2)}) collective-permute-start(bf16[48,768]{1,0:T(8,128)(2,1)S(1)} %get-tuple-element.55), channel_id=1, source_target_pairs={{0,2},{1,3},{2,4},{3,5},{4,6},{5,7},{6,0},{7,1},{8,10},{9,11},{10,... | collective-permute-start | bytes 221192 | tf_op jit(solution)/shard_map/ppermute | solution.py:469
  30.0 0.0 collective-permute-done.5
  30.0 0.0 collective-permute-start.6
  30.0 1.2 %collective-permute-done.6.passed_ref = s32[32,128]{1,0:T(8,128)S(1)} collective-permute-done((s32[32,128]{1,0:T(8,128)S(1)}, s32[32,128]{1,0:T(8,128)S(1)}, u32[]{:S(2)}, u32[]{:S(2)}) %collective-permute-start.6) | collective-permute-done | bytes 16416 | tf_op jit(solution)/shard_map/ppermute | solution.py:460
  31.2 0.3 shard_map.85.pick_ref
  31.4 0.0 collective-permute-done.14.refs_1_
  31.4 3.1 %collective-permute-done.15.refs_2_ = bf16[48,768]{1,0:T(8,128)(2,1)S(1)} collective-permute-done((bf16[48,768]{1,0:T(8,128)(2,1)S(1)}, bf16[48,768]{1,0:T(8,128)(2,1)S(1)}, u32[]{:S(2)}, u32[]{:S(2)}) %collective-permute-start.15) | collective-permute-done | bytes 73760 | tf_op jit(solution)/shard_map/ppermute | solution.py:469
  34.6 0.9 %collective-permute-done.16.refs_3_ = bf16[48,768]{1,0:T(8,128)(2,1)S(1)} collective-permute-done((bf16[48,768]{1,0:T(8,128)(2,1)S(1)}, bf16[48,768]{1,0:T(8,128)(2,1)S(1)}, u32[]{:S(2)}, u32[]{:S(2)}) %collective-permute-start.16) | collective-permute-done | bytes 73760 | tf_op jit(solution)/shard_map/ppermute | solution.py:469
  35.5 1.8 %shard_map.87 = (bf16[192,768]{1,0:T(8,128)(2,1)}, bf16[128,768]{1,0:T(8,128)(2,1)}, bf16[32,3,2,768]{3,2,1,0:T(2,128)(2,1)}) custom-call(bf16[128,768]{1,0:T(8,128)(2,1)S(1)} %get-tuple-element.40.refs_4_.features_ref, bf16[128,128]{1,0:T(8,128)(2,1)S(1)} %get-tuple-element.41.near_ref, bf16[128,200]{1,0:T(8,128)(2,1)S(1)} %get-tuple-element.42.far_ref, ...), custom_call_target="tpu_custom_call" | custom-call | flops 100663296 | bytes 1411072 | tf_op jit(solution)/shard_map/pallas_call | solution.py:56
  37.3 2.6 %all-to-all-start = ((bf16[32,3,2,768]{3,2,1,0:T(2,128)(2,1)}), bf16[32,3,2,768]{3,2,1,0:T(2,128)(2,1)S(1)}, u32[]{:S(2)}, u32[]{:S(2)}) async-start(bf16[32,3,2,768]{3,2,1,0:T(2,128)(2,1)} %get-tuple-element.63), calls=%async_computation | async-start | bytes 589824 | tf_op jit(solution)/shard_map/all_to_all | solution.py:491
  39.9 5.0 %shard_map.88 = (f32[128,1024]{1,0:T(8,128)}, bf16[128,128]{1,0:T(8,128)(2,1)}, bf16[192,1024]{1,0:T(8,128)(2,1)S(1)}, bf16[128,200]{1,0:T(8,128)(2,1)S(1)}, bf1...) custom-call(bf16[768,1024]{1,0:T(8,128)(2,1)} %self_one_hbm.1, bf16[768,1024]{1,0:T(8,128)(2,1)} %neigh_one_hbm.1, ...), custom_call_target="tpu_custom_call" | custom-call | flops 1275068416 | bytes 11751936 | tf_op jit(solution)/shard_map/pallas_call | solution.py:56
  44.9 6.3 %all-to-all-done.answer_ref = bf16[32,3,2,768]{3,2,1,0:T(2,128)(2,1)S(1)} async-done(((bf16[32,3,2,768]{3,2,1,0:T(2,128)(2,1)}), bf16[32,3,2,768]{3,2,1,0:T(2,128)(2,1)S(1)}, u32[]{:S(2)}, u32[]{:S(2)}) %all-to-all-start) | async-done | bytes 294944 | tf_op jit(solution)/shard_map/all_to_all | solution.py:491
  51.2 0.0 copy-start
  51.2 2.2 %shard_map.89 = (bf16[32,1024]{1,0:T(8,128)(2,1)S(1)}, bf16[32,1024]{1,0:T(8,128)(2,1)S(1)}, bf16[32,1024]{1,0:T(8,128)(2,1)S(1)}, bf16[32,1024]{1,0:T(8,128)(2,1)S(1)}) custom-call(bf16[1024,1024]{1,0:T(8,128)(2,1)} %neigh_two_hbm.3, f32[128,1024]{1,0:T(8,128)} %get-tuple-element.59.final_hbm, bf16[768,1024]{1,0:T(8,128)(2,1)S(1)} %get-tuple-element.60.neigh_one_ref, ...), custom_call_target="tpu_custom_call" | custom-call | flops 620756992 | bytes 6244352 | tf_op jit(solution)/shard_map/pallas_call | solution.py:56
  53.4 0.1 collective-permute-start.17
  53.5 0.2 collective-permute-start.18
  53.8 3.6 %collective-permute-start.19 = (bf16[32,1024]{1,0:T(8,128)(2,1)S(1)}, bf16[32,1024]{1,0:T(8,128)(2,1)S(1)}, u32[]{:S(2)}, u32[]{:S(2)}) collective-permute-start(bf16[32,1024]{1,0:T(8,128)(2,1)S(1)} %get-tuple-element.68), channel_id=1, source_target_pairs={{0,6},{1,7},{2,0},{3,1},{4,2},{5,3},{6,4},{7,5},{8,14},{9,15},{10,... | collective-permute-start | bytes 196616 | tf_op jit(solution)/shard_map/ppermute | solution.py:531
  57.3 3.0 %collective-permute-done.17.refs_1_ = bf16[32,1024]{1,0:T(8,128)(2,1)S(1)} collective-permute-done((bf16[32,1024]{1,0:T(8,128)(2,1)S(1)}, bf16[32,1024]{1,0:T(8,128)(2,1)S(1)}, u32[]{:S(2)}, u32[]{:S(2)}) %collective-permute-start.17) | collective-permute-done | bytes 65568 | tf_op jit(solution)/shard_map/ppermute | solution.py:531
  60.3 1.8 %collective-permute-done.18.refs_2_ = bf16[32,1024]{1,0:T(8,128)(2,1)S(1)} collective-permute-done((bf16[32,1024]{1,0:T(8,128)(2,1)S(1)}, bf16[32,1024]{1,0:T(8,128)(2,1)S(1)}, u32[]{:S(2)}, u32[]{:S(2)}) %collective-permute-start.18) | collective-permute-done | bytes 65568 | tf_op jit(solution)/shard_map/ppermute | solution.py:531
  62.1 0.0 collective-permute-done.19.refs_3_
  62.1 0.0 copy-done
  62.1 0.9 %shard_map.90 = bf16[128,1024]{1,0:T(8,128)(2,1)} custom-call(bf16[128,128]{1,0:T(8,128)(2,1)S(1)} %copy-done, bf16[32,1024]{1,0:T(8,128)(2,1)S(1)} %get-tuple-element.65.refs_0_, bf16[32,1024]{1,0:T(8,128)(2,1)S(1)} %collective-permute-done.17.refs_1_, bf16[32,1024]{1,0:T(8,128)(2,1)S(1)} %collective-permute-done.18.refs_2_, ...), custom_call_target="tpu_custom_call" | custom-call | flops 33554432 | bytes 557056 | tf_op jit(solution)/shard_map/pallas_call | solution.py:56
  (4 shorter events, 0.0 us)
Async XLA Ops:
  0.0 20.4 %collective-permute-start.10 = (bf16[128,768]{1,0:T(8,128)(2,1)}, bf16[128,768]{1,0:T(8,128)(2,1)S(1)}, u32[]{:S(2)}, u32[]{:S(2)}) collective-permute-start(bf16[128,768]{1,0:T(8,128)(2,1)} %features_hbm.3), channel_id=1, source_target_pairs={{0,16},{8,24},{16,0},{24,8},{1,17},{9,25},{17,1},{25,9},{2,18},{10... | collective-permute-start | bytes 589832 | tf_op jit(solution)/shard_map/ppermute | solution.py:421
  3.0 17.5 %collective-permute-start.8 = (bf16[128,768]{1,0:T(8,128)(2,1)}, bf16[128,768]{1,0:T(8,128)(2,1)S(1)}, u32[]{:S(2)}, u32[]{:S(2)}) collective-permute-start(bf16[128,768]{1,0:T(8,128)(2,1)} %features_hbm.3), channel_id=1, source_target_pairs={{0,8},{8,0},{16,24},{24,16},{1,9},{9,1},{17,25},{25,17},{2,10},{10... | collective-permute-start | bytes 589832 | tf_op jit(solution)/shard_map/ppermute | solution.py:421
  4.5 16.5 %collective-permute-start.12 = (bf16[128,768]{1,0:T(8,128)(2,1)}, bf16[128,768]{1,0:T(8,128)(2,1)S(1)}, u32[]{:S(2)}, u32[]{:S(2)}) collective-permute-start(bf16[128,768]{1,0:T(8,128)(2,1)} %features_hbm.3), channel_id=1, source_target_pairs={{0,24},{8,16},{16,8},{24,0},{1,25},{9,17},{17,9},{25,1},{2,26},{10... | collective-permute-start | bytes 589832 | tf_op jit(solution)/shard_map/ppermute | solution.py:421
  5.6 5.7 %collective-permute-start = (s32[8,128]{1,0:T(8,128)S(1)}, s32[8,128]{1,0:T(8,128)S(1)}, u32[]{:S(2)}, u32[]{:S(2)}) collective-permute-start(s32[8,128]{1,0:T(8,128)S(1)} %get-tuple-element.44), channel_id=1, source_target_pairs={{0,2},{1,3},{2,4},{3,5},{4,6},{5,7},{6,0},{7,1},{8,10},{9,11},{10,... | collective-permute-start | bytes 12296 | tf_op jit(solution)/shard_map/ppermute | solution.py:436
  7.7 6.6 %collective-permute-start.1 = (s32[8,128]{1,0:T(8,128)S(1)}, s32[8,128]{1,0:T(8,128)S(1)}, u32[]{:S(2)}, u32[]{:S(2)}) collective-permute-start(s32[8,128]{1,0:T(8,128)S(1)} %get-tuple-element.45), channel_id=1, source_target_pairs={{0,4},{1,5},{2,6},{3,7},{4,0},{5,1},{6,2},{7,3},{8,12},{9,13},{10,... | collective-permute-start | bytes 12296 | tf_op jit(solution)/shard_map/ppermute | solution.py:436
  11.3 3.6 %collective-permute-start.2 = (s32[8,128]{1,0:T(8,128)S(1)}, s32[8,128]{1,0:T(8,128)S(1)}, u32[]{:S(2)}, u32[]{:S(2)}) collective-permute-start(s32[8,128]{1,0:T(8,128)S(1)} %get-tuple-element.46), channel_id=1, source_target_pairs={{0,6},{1,7},{2,0},{3,1},{4,2},{5,3},{6,4},{7,5},{8,14},{9,15},{10,... | collective-permute-start | bytes 12296 | tf_op jit(solution)/shard_map/ppermute | solution.py:436
  14.4 10.6 %collective-permute-start.7 = (bf16[128,768]{1,0:T(8,128)(2,1)}, bf16[128,768]{1,0:T(8,128)(2,1)S(1)}, u32[]{:S(2)}, u32[]{:S(2)}) collective-permute-start(bf16[128,768]{1,0:T(8,128)(2,1)} %features_hbm.3), channel_id=1, source_target_pairs={{0,1},{1,0},{2,3},{3,2},{4,5},{5,4},{6,7},{7,6},{8,9},{9,8},{10,11... | collective-permute-start | bytes 589832 | tf_op jit(solution)/shard_map/ppermute | solution.py:422
  15.1 3.6 %collective-permute-start.3 = (s32[8,128]{1,0:T(8,128)S(1)}, s32[8,128]{1,0:T(8,128)S(1)}, u32[]{:S(2)}, u32[]{:S(2)}) collective-permute-start(s32[8,128]{1,0:T(8,128)S(1)} %get-tuple-element.48), channel_id=1, source_target_pairs={{0,8},{8,0},{16,24},{24,16},{1,9},{9,1},{17,25},{25,17},{2,10},{10... | collective-permute-start | bytes 12296 | tf_op jit(solution)/shard_map/ppermute | solution.py:459
  18.7 3.6 %collective-permute-start.4 = (s32[8,128]{1,0:T(8,128)S(1)}, s32[8,128]{1,0:T(8,128)S(1)}, u32[]{:S(2)}, u32[]{:S(2)}) collective-permute-start(s32[8,128]{1,0:T(8,128)S(1)} %get-tuple-element.49), channel_id=1, source_target_pairs={{0,16},{8,24},{16,0},{24,8},{1,17},{9,25},{17,1},{25,9},{2,18},{10... | collective-permute-start | bytes 12296 | tf_op jit(solution)/shard_map/ppermute | solution.py:459
  20.4 4.5 %collective-permute-start.11 = (bf16[128,768]{1,0:T(8,128)(2,1)S(1)}, bf16[128,768]{1,0:T(8,128)(2,1)S(1)}, u32[]{:S(2)}, u32[]{:S(2)}) collective-permute-start(bf16[128,768]{1,0:T(8,128)(2,1)S(1)} %collective-permute-done.10.refs_8_), channel_id=1, source_target_pairs={{0,1},{1,0},{2,3},{3,2},{4,5},{5,4},{6,7},{7,6},{8,9},{9,8},{10,11... | collective-permute-start | bytes 589832 | tf_op jit(solution)/shard_map/ppermute | solution.py:422
  20.4 4.5 %collective-permute-start.9 = (bf16[128,768]{1,0:T(8,128)(2,1)S(1)}, bf16[128,768]{1,0:T(8,128)(2,1)S(1)}, u32[]{:S(2)}, u32[]{:S(2)}) collective-permute-start(bf16[128,768]{1,0:T(8,128)(2,1)S(1)} %collective-permute-done.8.refs_6_), channel_id=1, source_target_pairs={{0,1},{1,0},{2,3},{3,2},{4,5},{5,4},{6,7},{7,6},{8,9},{9,8},{10,11... | collective-permute-start | bytes 589832 | tf_op jit(solution)/shard_map/ppermute | solution.py:422
  21.0 4.0 %collective-permute-start.13 = (bf16[128,768]{1,0:T(8,128)(2,1)S(1)}, bf16[128,768]{1,0:T(8,128)(2,1)S(1)}, u32[]{:S(2)}, u32[]{:S(2)}) collective-permute-start(bf16[128,768]{1,0:T(8,128)(2,1)S(1)} %collective-permute-done.12.refs_10_), channel_id=1, source_target_pairs={{0,1},{1,0},{2,3},{3,2},{4,5},{5,4},{6,7},{7,6},{8,9},{9,8},{10,11... | collective-permute-start | bytes 589832 | tf_op jit(solution)/shard_map/ppermute | solution.py:422
  22.3 7.7 %collective-permute-start.5 = (s32[8,128]{1,0:T(8,128)S(1)}, s32[8,128]{1,0:T(8,128)S(1)}, u32[]{:S(2)}, u32[]{:S(2)}) collective-permute-start(s32[8,128]{1,0:T(8,128)S(1)} %get-tuple-element.50), channel_id=1, source_target_pairs={{0,24},{8,16},{16,8},{24,0},{1,25},{9,17},{17,9},{25,1},{2,26},{10... | collective-permute-start | bytes 12296 | tf_op jit(solution)/shard_map/ppermute | solution.py:459
  25.7 5.7 %collective-permute-start.14 = (bf16[48,768]{1,0:T(8,128)(2,1)S(1)}, bf16[48,768]{1,0:T(8,128)(2,1)S(1)}, u32[]{:S(2)}, u32[]{:S(2)}) collective-permute-start(bf16[48,768]{1,0:T(8,128)(2,1)S(1)} %get-tuple-element.53), channel_id=1, source_target_pairs={{0,6},{1,7},{2,0},{3,1},{4,2},{5,3},{6,4},{7,5},{8,14},{9,15},{10,... | collective-permute-start | bytes 221192 | tf_op jit(solution)/shard_map/ppermute | solution.py:469
  29.3 5.3 %collective-permute-start.15 = (bf16[48,768]{1,0:T(8,128)(2,1)S(1)}, bf16[48,768]{1,0:T(8,128)(2,1)S(1)}, u32[]{:S(2)}, u32[]{:S(2)}) collective-permute-start(bf16[48,768]{1,0:T(8,128)(2,1)S(1)} %get-tuple-element.54), channel_id=1, source_target_pairs={{0,4},{1,5},{2,6},{3,7},{4,0},{5,1},{6,2},{7,3},{8,12},{9,13},{10,... | collective-permute-start | bytes 221192 | tf_op jit(solution)/shard_map/ppermute | solution.py:469
  29.3 6.2 %collective-permute-start.16 = (bf16[48,768]{1,0:T(8,128)(2,1)S(1)}, bf16[48,768]{1,0:T(8,128)(2,1)S(1)}, u32[]{:S(2)}, u32[]{:S(2)}) collective-permute-start(bf16[48,768]{1,0:T(8,128)(2,1)S(1)} %get-tuple-element.55), channel_id=1, source_target_pairs={{0,2},{1,3},{2,4},{3,5},{4,6},{5,7},{6,0},{7,1},{8,10},{9,11},{10,... | collective-permute-start | bytes 221192 | tf_op jit(solution)/shard_map/ppermute | solution.py:469
  30.0 1.2 %collective-permute-start.6 = (s32[32,128]{1,0:T(8,128)S(1)}, s32[32,128]{1,0:T(8,128)S(1)}, u32[]{:S(2)}, u32[]{:S(2)}) collective-permute-start(s32[32,128]{1,0:T(8,128)S(1)} %constant_dynamic-update-slice_fusion.kept_ref), channel_id=1, source_target_pairs={{0,1},{1,0},{2,3},{3,2},{4,5},{5,4},{6,7},{7,6},{8,9},{9,8},{10,11... | collective-permute-start | bytes 49160 | tf_op jit(solution)/shard_map/ppermute | solution.py:460
  37.3 13.9 %all-to-all-start = ((bf16[32,3,2,768]{3,2,1,0:T(2,128)(2,1)}), bf16[32,3,2,768]{3,2,1,0:T(2,128)(2,1)S(1)}, u32[]{:S(2)}, u32[]{:S(2)}) async-start(bf16[32,3,2,768]{3,2,1,0:T(2,128)(2,1)} %get-tuple-element.63), calls=%async_computation | async-start | bytes 589824 | tf_op jit(solution)/shard_map/all_to_all | solution.py:491
  51.2 10.9 %copy-start = (bf16[128,128]{1,0:T(8,128)(2,1)S(1)}, bf16[128,128]{1,0:T(8,128)(2,1)}, u32[]{:S(2)}) copy-start(bf16[128,128]{1,0:T(8,128)(2,1)} %get-tuple-element.58.place_ref) | copy-start | bytes 98308
  53.4 6.9 %collective-permute-start.17 = (bf16[32,1024]{1,0:T(8,128)(2,1)S(1)}, bf16[32,1024]{1,0:T(8,128)(2,1)S(1)}, u32[]{:S(2)}, u32[]{:S(2)}) collective-permute-start(bf16[32,1024]{1,0:T(8,128)(2,1)S(1)} %get-tuple-element.66), channel_id=1, source_target_pairs={{0,2},{1,3},{2,4},{3,5},{4,6},{5,7},{6,0},{7,1},{8,10},{9,11},{10,... | collective-permute-start | bytes 196616 | tf_op jit(solution)/shard_map/ppermute | solution.py:531
  53.5 8.6 %collective-permute-start.18 = (bf16[32,1024]{1,0:T(8,128)(2,1)S(1)}, bf16[32,1024]{1,0:T(8,128)(2,1)S(1)}, u32[]{:S(2)}, u32[]{:S(2)}) collective-permute-start(bf16[32,1024]{1,0:T(8,128)(2,1)S(1)} %get-tuple-element.67), channel_id=1, source_target_pairs={{0,4},{1,5},{2,6},{3,7},{4,0},{5,1},{6,2},{7,3},{8,12},{9,13},{10,... | collective-permute-start | bytes 196616 | tf_op jit(solution)/shard_map/ppermute | solution.py:531
  53.8 8.4 %collective-permute-start.19 = (bf16[32,1024]{1,0:T(8,128)(2,1)S(1)}, bf16[32,1024]{1,0:T(8,128)(2,1)S(1)}, u32[]{:S(2)}, u32[]{:S(2)}) collective-permute-start(bf16[32,1024]{1,0:T(8,128)(2,1)S(1)} %get-tuple-element.68), channel_id=1, source_target_pairs={{0,6},{1,7},{2,0},{3,1},{4,2},{5,3},{6,4},{7,5},{8,14},{9,15},{10,... | collective-permute-start | bytes 196616 | tf_op jit(solution)/shard_map/ppermute | solution.py:531
where the time goes:
time: 63.4 us; the launch traced here: 63 us
  starting transfers between devices  28.8 us (45%)
  waiting for transfers between devices  21 us (33%)
  Pallas kernels  13.1 us (21%)
    pallas_call x9, Pallas kernels, call(): pl.pallas_call(kernel, out_shape=outs if single else (*(pltpu.HBM(a.shape...  13.1 us
    ppermute x3, starting transfers between devices, compute(): lax.ppermute(asks[q], 'dev', shifts(2 * q))  6.71 us
    all_to_all x1, waiting for transfers between devices, compute(): answer_two = lax.all_to_all(reply_two, BOTH, 0, 0, tiled=True)  6.31 us
    ppermute x3, starting transfers between devices, compute(): lax.ppermute(by_mate[m], 'grp', across(m))  6.22 us
    ppermute x3, waiting for transfers between devices, compute(): arrived.append(lax.ppermute(finals[q], 'dev', shifts(2 * q)))  4.8 us
    ppermute x3, starting transfers between devices, compute(): lax.ppermute(features, 'grp', across(m))  4.49 us
    ppermute x3, starting transfers between devices, compute(): lax.ppermute(replies[q], 'dev', shifts(-2 * q))  4.26 us
    ppermute x3, waiting for transfers between devices, compute(): lax.ppermute(replies[q], 'dev', shifts(-2 * q))  4.05 us
  transfers between devices with their start and end apart: 21, of which 10 were waited for; matrix products, arithmetic and copies ran while one was open for 0% of the time, Pallas kernels for 13%

commit v1 on v0

--- a/solution.py
+++ b/solution.py
@@ -244,17 +244,31 @@
         ref[...] = rows[q * block : (q + 1) * block]
 
 
-def pick_kernel(members, kept_ref, passed_ref, pick_ref):
+def line_kernel(kept_ref, passed_ref, *refs):
+    steps = len(refs)
     kept = kept_ref[...]
     peers = kept.shape[0]
-    steps = members // 2
     half = divide(iota(kept.shape, 0), steps)
     wanted = jnp.where((half & 1) == 0, kept, passed_ref[...])
+    mates = peers // steps
+    line = iota((peers, peers), 0)
+    step = divide(line, mates)
+    pick = bits(iota((peers, peers), 1) == (line - step * mates) * steps + step).astype(BF16)
+    sorted_rows = dot(pick, wanted.astype(F32).astype(BF16)).astype(I32)
+    for q, ref in enumerate(refs):
+        ref[...] = sorted_rows[q * mates : (q + 1) * mates]
+
+
+def pick_kernel(members, *refs):
+    wanted_refs, pick_ref = refs[:-1], refs[-1]
+    wanted = jnp.concatenate([ref[...] for ref in wanted_refs], axis=0)
+    peers = wanted.shape[0]
+    steps = members // 2
     size = peers * CAP
     line = iota((size, size), 0)
     device = divide(line, CAP)
     step, group, core = apart(device, members)
-    row = (2 * group + core) * steps + wrap(-step, steps)
+    row = wrap(-step, steps) * (peers // steps) + 2 * group + core
     order = bits(iota((size, size), 1) == (line - device * CAP) * peers + row).astype(BF16)
     pick_ref[...] = picks_of(wanted, order)
 
@@ -452,7 +466,7 @@
         functools.partial(sort_kernel, groups),
         tuple(shape((2 * steps, rows), I32) for _ in range(groups)),
         (),
-        asked,
+        asks,
         [],
         2 * peers * peers * rows,
     )
@@ -467,13 +481,17 @@
         2 * size * rows * mates * width_in,
     )
     answers = [replies[0]] + [lax.ppermute(replies[q], "dev", shifts(-2 * q)) for q in range(1, steps)]
-    pick = call(
-        functools.partial(pick_kernel, members),
-        shape((size, rows), BF16),
+    lines = call(
+        line_kernel,
+        tuple(shape((mates, rows), I32) for _ in range(steps)),
         (),
         (kept_asks, passed_asks),
         [],
-        2 * size * size * rows,
+        2 * peers * peers * rows,
+    )
+    wanted = [lines[0]] + [lax.ppermute(lines[q], "dev", shifts(2 * q)) for q in range(1, steps)]
+    pick = call(
+        functools.partial(pick_kernel, members), shape((size, rows), BF16), (), wanted, [], 2 * size * size * rows
     )
     kept, mean, reply_two = call(
         layer_one_kernel,

time: 63.4 us -> 69.7 us (1.099)
  starting transfers between devices: 28.8 us -> 35.5 us
    ppermute x0 -> x3, starting transfers between devices: none -> 5.13 us  [compute(): lax.ppermute(lines[q], 'dev', shifts(2 * q))]
    ppermute x3, waiting for transfers between devices: 4.05 us -> 0.01 us  [compute(): lax.ppermute(replies[q], 'dev', shifts(-2 * q))]
    ppermute x0 -> x3, waiting for transfers between devices: none -> 3.88 us  [compute(): lax.ppermute(lines[q], 'dev', shifts(2 * q))]
    all_to_all x1, starting transfers between devices: 2.6 us -> 4.02 us  [compute(): answer_two = lax.all_to_all(reply_two, BOTH, 0, 0, tiled=True)]
    ppermute x3, waiting for transfers between devices: 3.1 us -> 2.08 us  [compute(): lax.ppermute(by_mate[m], 'grp', across(m))]
    ppermute x3, waiting for transfers between devices: 1.52 us -> 2.22 us  [compute(): lax.ppermute(asks[q], 'dev', shifts(2 * q))]
    pallas_call x9 -> x10, Pallas kernels: 13.1 us -> 13.2 us  [call(): pl.pallas_call(kernel, out_shape=outs if single else (*(pltpu.HBM(a.shape...]
  transfers between devices with their start and end apart: 21 -> 24, of which waited for: 10 -> 11; matrix products, arithmetic and copies ran while one was open for 0% -> 0% of each run, Pallas kernels for 13% -> 12%
where the time goes in v1:
time: 69.7 us; the launch traced here: 69.4 us
  starting transfers between devices  35.5 us (51%)
  waiting for transfers between devices  20.5 us (29%)
  Pallas kernels  13.2 us (19%)
    pallas_call x10, Pallas kernels, call(): pl.pallas_call(kernel, out_shape=outs if single else (*(pltpu.HBM(a.shape...  13.2 us
    ppermute x3, starting transfers between devices, compute(): lax.ppermute(asks[q], 'dev', shifts(2 * q))  7.24 us
    all_to_all x1, waiting for transfers between devices, compute(): answer_two = lax.all_to_all(reply_two, BOTH, 0, 0, tiled=True)  6.34 us
    ppermute x3, starting transfers between devices, compute(): lax.ppermute(by_mate[m], 'grp', across(m))  5.84 us
    ppermute x3, starting transfers between devices, compute(): lax.ppermute(lines[q], 'dev', shifts(2 * q))  5.13 us
    ppermute x3, waiting for transfers between devices, compute(): arrived.append(lax.ppermute(finals[q], 'dev', shifts(2 * q)))  4.79 us
    ppermute x3, starting transfers between devices, compute(): lax.ppermute(features, 'grp', across(m))  4.49 us
    ppermute x3, starting transfers between devices, compute(): lax.ppermute(replies[q], 'dev', shifts(-2 * q))  4.3 us
  transfers between devices with their start and end apart: 24, of which 11 were waited for; matrix products, arithmetic and copies ran while one was open for 0% of the time, Pallas kernels for 12%

profile of v1, /device:TPU:0, one launch (start us, length us, event | category | flops | bytes accessed | tf_op | source)
XLA Modules:
  0.0 69.4 jit_solution(9955898087728384608)
XLA Ops:
  0.0 3.0 %collective-permute-start.13 = (bf16[128,768]{1,0:T(8,128)(2,1)}, bf16[128,768]{1,0:T(8,128)(2,1)S(1)}, u32[]{:S(2)}, u32[]{:S(2)}) collective-permute-start(bf16[128,768]{1,0:T(8,128)(2,1)} %features_hbm.3), channel_id=1, source_target_pairs={{0,16},{8,24},{16,0},{24,8},{1,17},{9,25},{17,1},{25,9},{2,18},{10... | collective-permute-start | bytes 589832 | tf_op jit(solution)/shard_map/ppermute | solution.py:435
  3.0 1.5 %collective-permute-start.11 = (bf16[128,768]{1,0:T(8,128)(2,1)}, bf16[128,768]{1,0:T(8,128)(2,1)S(1)}, u32[]{:S(2)}, u32[]{:S(2)}) collective-permute-start(bf16[128,768]{1,0:T(8,128)(2,1)} %features_hbm.3), channel_id=1, source_target_pairs={{0,8},{8,0},{16,24},{24,16},{1,9},{9,1},{17,25},{25,17},{2,10},{10... | collective-permute-start | bytes 589832 | tf_op jit(solution)/shard_map/ppermute | solution.py:435
  4.5 0.0 collective-permute-start.15
  4.5 1.1 %shard_map.82 = (s32[25,128]{1,0:T(8,128)S(1)}, s32[25,128]{1,0:T(8,128)S(1)}, s32[2,32,128]{2,1,0:T(8,128)S(1)}, s32[8,128]{1,0:T(8,128)S(1)}, s32[8,128]{1,0:T...) custom-call(s32[25,128]{1,0:T(8,128)} %bitcast.3, s32[25,128]{1,0:T(8,128)} %bitcast.4, s32[1,128]{1,0:T(1,128)} %bitcast.5), custom_call_target="tpu_custom_call" | custom-call | flops 1048576 | bytes 100864 | tf_op jit(solution)/shard_map/pallas_call | solution.py:56
  5.6 2.1 %collective-permute-start.7 = (s32[8,128]{1,0:T(8,128)S(1)}, s32[8,128]{1,0:T(8,128)S(1)}, u32[]{:S(2)}, u32[]{:S(2)}) collective-permute-start(s32[8,128]{1,0:T(8,128)S(1)} %get-tuple-element.48.refs_1_), channel_id=1, source_target_pairs={{0,2},{1,3},{2,4},{3,5},{4,6},{5,7},{6,0},{7,1},{8,10},{9,11},{10,... | collective-permute-start | bytes 12296 | tf_op jit(solution)/shard_map/ppermute | solution.py:450
  7.7 2.6 %collective-permute-start.8 = (s32[8,128]{1,0:T(8,128)S(1)}, s32[8,128]{1,0:T(8,128)S(1)}, u32[]{:S(2)}, u32[]{:S(2)}) collective-permute-start(s32[8,128]{1,0:T(8,128)S(1)} %get-tuple-element.49.refs_2_), channel_id=1, source_target_pairs={{0,4},{1,5},{2,6},{3,7},{4,0},{5,1},{6,2},{7,3},{8,12},{9,13},{10,... | collective-permute-start | bytes 12296 | tf_op jit(solution)/shard_map/ppermute | solution.py:450
  10.3 0.1 shard_map.84
  10.4 0.9 %collective-permute-done.7.refs_1_ = s32[8,128]{1,0:T(8,128)S(1)} collective-permute-done((s32[8,128]{1,0:T(8,128)S(1)}, s32[8,128]{1,0:T(8,128)S(1)}, u32[]{:S(2)}, u32[]{:S(2)}) %collective-permute-start.7) | collective-permute-done | bytes 4128 | tf_op jit(solution)/shard_map/ppermute | solution.py:450
  11.3 1.7 %collective-permute-start = (s32[8,128]{1,0:T(8,128)S(1)}, s32[8,128]{1,0:T(8,128)S(1)}, u32[]{:S(2)}, u32[]{:S(2)}) collective-permute-start(s32[8,128]{1,0:T(8,128)S(1)} %get-tuple-element.52), channel_id=1, source_target_pairs={{0,8},{8,0},{16,24},{24,16},{1,9},{9,1},{17,25},{25,17},{2,10},{10... | collective-permute-start | bytes 12296 | tf_op jit(solution)/shard_map/ppermute | solution.py:473
  13.0 1.0 %shard_map.83 = (bf16[128,128]{1,0:T(8,128)(2,1)S(1)}, bf16[128,200]{1,0:T(8,128)(2,1)S(1)}, bf16[192,192]{1,0:T(8,128)(2,1)S(1)}, bf16[128,768]{1,0:T(8,128)(2,1)S(1)}) custom-call(bf16[128,768]{1,0:T(8,128)(2,1)} %features_hbm.3, s32[25,128]{1,0:T(8,128)S(1)} %get-tuple-element.41.key_ref, s32[25,128]{1,0:T(8,128)S(1)} %get-tuple-element.42.local_ref, ...), custom_call_target="tpu_custom_call" | custom-call | flops 9437184 | bytes 609280 | tf_op jit(solution)/shard_map/pallas_call | solution.py:56
  14.0 0.0 collective-permute-done.8.refs_2_
  14.0 0.1 collective-permute-start.10
  14.1 0.8 %collective-permute-done = s32[8,128]{1,0:T(8,128)S(1)} collective-permute-done((s32[8,128]{1,0:T(8,128)S(1)}, s32[8,128]{1,0:T(8,128)S(1)}, u32[]{:S(2)}, u32[]{:S(2)}) %collective-permute-start) | collective-permute-done | bytes 4128 | tf_op jit(solution)/shard_map/ppermute | solution.py:473
  14.9 1.7 %collective-permute-start.1 = (s32[8,128]{1,0:T(8,128)S(1)}, s32[8,128]{1,0:T(8,128)S(1)}, u32[]{:S(2)}, u32[]{:S(2)}) collective-permute-start(s32[8,128]{1,0:T(8,128)S(1)} %get-tuple-element.53), channel_id=1, source_target_pairs={{0,16},{8,24},{16,0},{24,8},{1,17},{9,25},{17,1},{25,9},{2,18},{10... | collective-permute-start | bytes 12296 | tf_op jit(solution)/shard_map/ppermute | solution.py:473
  16.7 0.0 collective-permute-done.13.refs_8_
  16.7 0.0 collective-permute-start.14
  16.7 0.0 collective-permute-done.11.refs_6_
  16.7 0.5 collective-permute-start.12
  17.2 0.0 collective-permute-done.15.refs_10_
  17.2 0.1 collective-permute-start.16
  17.3 1.3 %collective-permute-done.1 = s32[8,128]{1,0:T(8,128)S(1)} collective-permute-done((s32[8,128]{1,0:T(8,128)S(1)}, s32[8,128]{1,0:T(8,128)S(1)}, u32[]{:S(2)}, u32[]{:S(2)}) %collective-permute-start.1) | collective-permute-done | bytes 4128 | tf_op jit(solution)/shard_map/ppermute | solution.py:473
  18.5 2.5 %collective-permute-start.9 = (s32[8,128]{1,0:T(8,128)S(1)}, s32[8,128]{1,0:T(8,128)S(1)}, u32[]{:S(2)}, u32[]{:S(2)}) collective-permute-start(s32[8,128]{1,0:T(8,128)S(1)} %get-tuple-element.50.refs_3_), channel_id=1, source_target_pairs={{0,6},{1,7},{2,0},{3,1},{4,2},{5,3},{6,4},{7,5},{8,14},{9,15},{10,... | collective-permute-start | bytes 12296 | tf_op jit(solution)/shard_map/ppermute | solution.py:450
  21.1 1.3 %collective-permute-done.9.refs_3_ = s32[8,128]{1,0:T(8,128)S(1)} collective-permute-done((s32[8,128]{1,0:T(8,128)S(1)}, s32[8,128]{1,0:T(8,128)S(1)}, u32[]{:S(2)}, u32[]{:S(2)}) %collective-permute-start.9) | collective-permute-done | bytes 4128 | tf_op jit(solution)/shard_map/ppermute | solution.py:450
  22.4 2.4 %collective-permute-start.2 = (s32[8,128]{1,0:T(8,128)S(1)}, s32[8,128]{1,0:T(8,128)S(1)}, u32[]{:S(2)}, u32[]{:S(2)}) collective-permute-start(s32[8,128]{1,0:T(8,128)S(1)} %get-tuple-element.54), channel_id=1, source_target_pairs={{0,24},{8,16},{16,8},{24,0},{1,25},{9,17},{17,9},{25,1},{2,26},{10... | collective-permute-start | bytes 12296 | tf_op jit(solution)/shard_map/ppermute | solution.py:473
  24.8 0.0 collective-permute-done.10.refs_5_
  24.8 0.0 collective-permute-done.14.refs_9_
  24.8 0.0 collective-permute-done.12.refs_7_
  24.8 0.0 collective-permute-done.16.refs_11_
  24.8 0.7 %shard_map.87 = (bf16[48,768]{1,0:T(8,128)(2,1)S(1)}, bf16[48,768]{1,0:T(8,128)(2,1)S(1)}, bf16[48,768]{1,0:T(8,128)(2,1)S(1)}, bf16[48,768]{1,0:T(8,128)(2,1)S(1)}) custom-call(bf16[192,192]{1,0:T(8,128)(2,1)S(1)} %get-tuple-element.59.order_ref, s32[8,128]{1,0:T(8,128)S(1)} %get-tuple-element.47.refs_0_, s32[8,128]{1,0:T(8,128)S(1)} %collective-permute-done.7.refs_1_, ...), custom_call_target="tpu_custom_call" | custom-call | flops 301989888 | bytes 1957888 | tf_op jit(solution)/shard_map/pallas_call | solution.py:56
  25.5 3.7 %collective-permute-start.17 = (bf16[48,768]{1,0:T(8,128)(2,1)S(1)}, bf16[48,768]{1,0:T(8,128)(2,1)S(1)}, u32[]{:S(2)}, u32[]{:S(2)}) collective-permute-start(bf16[48,768]{1,0:T(8,128)(2,1)S(1)} %get-tuple-element.61), channel_id=1, source_target_pairs={{0,6},{1,7},{2,0},{3,1},{4,2},{5,3},{6,4},{7,5},{8,14},{9,15},{10,... | collective-permute-start | bytes 221192 | tf_op jit(solution)/shard_map/ppermute | solution.py:483
  29.2 0.0 collective-permute-start.18
  29.2 0.6 collective-permute-start.19
  29.8 0.0 collective-permute-done.2
  29.8 0.0 collective-permute-start.3
  29.8 1.2 %collective-permute-done.3.passed_ref = s32[32,128]{1,0:T(8,128)S(1)} collective-permute-done((s32[32,128]{1,0:T(8,128)S(1)}, s32[32,128]{1,0:T(8,128)S(1)}, u32[]{:S(2)}, u32[]{:S(2)}) %collective-permute-start.3) | collective-permute-done | bytes 16416 | tf_op jit(solution)/shard_map/ppermute | solution.py:474
  31.0 0.1 shard_map.85
  31.2 2.8 %collective-permute-start.4 = (s32[8,128]{1,0:T(8,128)S(1)}, s32[8,128]{1,0:T(8,128)S(1)}, u32[]{:S(2)}, u32[]{:S(2)}) collective-permute-start(s32[8,128]{1,0:T(8,128)S(1)} %get-tuple-element.56), channel_id=1, source_target_pairs={{0,2},{1,3},{2,4},{3,5},{4,6},{5,7},{6,0},{7,1},{8,10},{9,11},{10,... | collective-permute-start | bytes 12296 | tf_op jit(solution)/shard_map/ppermute | solution.py:492
  34.0 0.9 %collective-permute-start.5 = (s32[8,128]{1,0:T(8,128)S(1)}, s32[8,128]{1,0:T(8,128)S(1)}, u32[]{:S(2)}, u32[]{:S(2)}) collective-permute-start(s32[8,128]{1,0:T(8,128)S(1)} %get-tuple-element.57), channel_id=1, source_target_pairs={{0,4},{1,5},{2,6},{3,7},{4,0},{5,1},{6,2},{7,3},{8,12},{9,13},{10,... | collective-permute-start | bytes 12296 | tf_op jit(solution)/shard_map/ppermute | solution.py:492
  34.9 1.7 %collective-permute-done.4.refs_1_ = s32[8,128]{1,0:T(8,128)S(1)} collective-permute-done((s32[8,128]{1,0:T(8,128)S(1)}, s32[8,128]{1,0:T(8,128)S(1)}, u32[]{:S(2)}, u32[]{:S(2)}) %collective-permute-start.4) | collective-permute-done | bytes 4128 | tf_op jit(solution)/shard_map/ppermute | solution.py:492
  36.6 1.4 %collective-permute-start.6 = (s32[8,128]{1,0:T(8,128)S(1)}, s32[8,128]{1,0:T(8,128)S(1)}, u32[]{:S(2)}, u32[]{:S(2)}) collective-permute-start(s32[8,128]{1,0:T(8,128)S(1)} %get-tuple-element.58), channel_id=1, source_target_pairs={{0,6},{1,7},{2,0},{3,1},{4,2},{5,3},{6,4},{7,5},{8,14},{9,15},{10,... | collective-permute-start | bytes 12296 | tf_op jit(solution)/shard_map/ppermute | solution.py:492
  37.9 0.6 collective-permute-done.5.refs_2_
  38.5 1.7 %collective-permute-done.6.refs_3_ = s32[8,128]{1,0:T(8,128)S(1)} collective-permute-done((s32[8,128]{1,0:T(8,128)S(1)}, s32[8,128]{1,0:T(8,128)S(1)}, u32[]{:S(2)}, u32[]{:S(2)}) %collective-permute-start.6) | collective-permute-done | bytes 4128 | tf_op jit(solution)/shard_map/ppermute | solution.py:492
  40.2 0.3 shard_map.86.pick_ref
  40.4 0.0 collective-permute-done.17.refs_1_
  40.4 0.0 collective-permute-done.18.refs_2_
  40.4 0.0 collective-permute-done.19.refs_3_
  40.5 1.8 %shard_map.88 = (bf16[192,768]{1,0:T(8,128)(2,1)}, bf16[128,768]{1,0:T(8,128)(2,1)}, bf16[32,3,2,768]{3,2,1,0:T(2,128)(2,1)}) custom-call(bf16[128,768]{1,0:T(8,128)(2,1)S(1)} %get-tuple-element.44.refs_4_.features_ref, bf16[128,128]{1,0:T(8,128)(2,1)S(1)} %get-tuple-element.45.near_ref, bf16[128,200]{1,0:T(8,128)(2,1)S(1)} %get-tuple-element.46.far_ref, ...), custom_call_target="tpu_custom_call" | custom-call | flops 100663296 | bytes 1411072 | tf_op jit(solution)/shard_map/pallas_call | solution.py:56
  42.3 4.0 %all-to-all-start = ((bf16[32,3,2,768]{3,2,1,0:T(2,128)(2,1)}), bf16[32,3,2,768]{3,2,1,0:T(2,128)(2,1)S(1)}, u32[]{:S(2)}, u32[]{:S(2)}) async-start(bf16[32,3,2,768]{3,2,1,0:T(2,128)(2,1)} %get-tuple-element.71), calls=%async_computation | async-start | bytes 589824 | tf_op jit(solution)/shard_map/all_to_all | solution.py:509
  46.3 5.0 %shard_map.89 = (f32[128,1024]{1,0:T(8,128)}, bf16[128,128]{1,0:T(8,128)(2,1)}, bf16[192,1024]{1,0:T(8,128)(2,1)S(1)}, bf16[128,200]{1,0:T(8,128)(2,1)S(1)}, bf1...) custom-call(bf16[768,1024]{1,0:T(8,128)(2,1)} %self_one_hbm.1, bf16[768,1024]{1,0:T(8,128)(2,1)} %neigh_one_hbm.1, ...), custom_call_target="tpu_custom_call" | custom-call | flops 1275068416 | bytes 11751936 | tf_op jit(solution)/shard_map/pallas_call | solution.py:56
  51.3 6.3 %all-to-all-done.answer_ref = bf16[32,3,2,768]{3,2,1,0:T(2,128)(2,1)S(1)} async-done(((bf16[32,3,2,768]{3,2,1,0:T(2,128)(2,1)}), bf16[32,3,2,768]{3,2,1,0:T(2,128)(2,1)S(1)}, u32[]{:S(2)}, u32[]{:S(2)}) %all-to-all-start) | async-done | bytes 294944 | tf_op jit(solution)/shard_map/all_to_all | solution.py:509
  57.6 0.0 copy-start
  57.6 2.2 %shard_map.90 = (bf16[32,1024]{1,0:T(8,128)(2,1)S(1)}, bf16[32,1024]{1,0:T(8,128)(2,1)S(1)}, bf16[32,1024]{1,0:T(8,128)(2,1)S(1)}, bf16[32,1024]{1,0:T(8,128)(2,1)S(1)}) custom-call(bf16[1024,1024]{1,0:T(8,128)(2,1)} %neigh_two_hbm.3, f32[128,1024]{1,0:T(8,128)} %get-tuple-element.67.final_hbm, bf16[768,1024]{1,0:T(8,128)(2,1)S(1)} %get-tuple-element.68.neigh_one_ref, ...), custom_call_target="tpu_custom_call" | custom-call | flops 620756992 | bytes 6244352 | tf_op jit(solution)/shard_map/pallas_call | solution.py:56
  59.8 0.1 collective-permute-start.20
  59.9 0.4 collective-permute-start.21
  60.3 3.4 %collective-permute-start.22 = (bf16[32,1024]{1,0:T(8,128)(2,1)S(1)}, bf16[32,1024]{1,0:T(8,128)(2,1)S(1)}, u32[]{:S(2)}, u32[]{:S(2)}) collective-permute-start(bf16[32,1024]{1,0:T(8,128)(2,1)S(1)} %get-tuple-element.76), channel_id=1, source_target_pairs={{0,6},{1,7},{2,0},{3,1},{4,2},{5,3},{6,4},{7,5},{8,14},{9,15},{10,... | collective-permute-start | bytes 196616 | tf_op jit(solution)/shard_map/ppermute | solution.py:549
  63.7 3.0 %collective-permute-done.20.refs_1_ = bf16[32,1024]{1,0:T(8,128)(2,1)S(1)} collective-permute-done((bf16[32,1024]{1,0:T(8,128)(2,1)S(1)}, bf16[32,1024]{1,0:T(8,128)(2,1)S(1)}, u32[]{:S(2)}, u32[]{:S(2)}) %collective-permute-start.20) | collective-permute-done | bytes 65568 | tf_op jit(solution)/shard_map/ppermute | solution.py:549
  66.7 1.8 %collective-permute-done.21.refs_2_ = bf16[32,1024]{1,0:T(8,128)(2,1)S(1)} collective-permute-done((bf16[32,1024]{1,0:T(8,128)(2,1)S(1)}, bf16[32,1024]{1,0:T(8,128)(2,1)S(1)}, u32[]{:S(2)}, u32[]{:S(2)}) %collective-permute-start.21) | collective-permute-done | bytes 65568 | tf_op jit(solution)/shard_map/ppermute | solution.py:549
  68.5 0.0 collective-permute-done.22.refs_3_
  68.5 0.0 copy-done
  68.5 0.9 %shard_map.91 = bf16[128,1024]{1,0:T(8,128)(2,1)} custom-call(bf16[128,128]{1,0:T(8,128)(2,1)S(1)} %copy-done, bf16[32,1024]{1,0:T(8,128)(2,1)S(1)} %get-tuple-element.73.refs_0_, bf16[32,1024]{1,0:T(8,128)(2,1)S(1)} %collective-permute-done.20.refs_1_, bf16[32,1024]{1,0:T(8,128)(2,1)S(1)} %collective-permute-done.21.refs_2_, ...), custom_call_target="tpu_custom_call" | custom-call | flops 33554432 | bytes 557056 | tf_op jit(solution)/shard_map/pallas_call | solution.py:56
  (4 shorter events, 0.0 us)
Async XLA Ops:
  0.0 16.7 %collective-permute-start.13 = (bf16[128,768]{1,0:T(8,128)(2,1)}, bf16[128,768]{1,0:T(8,128)(2,1)S(1)}, u32[]{:S(2)}, u32[]{:S(2)}) collective-permute-start(bf16[128,768]{1,0:T(8,128)(2,1)} %features_hbm.3), channel_id=1, source_target_pairs={{0,16},{8,24},{16,0},{24,8},{1,17},{9,25},{17,1},{25,9},{2,18},{10... | collective-permute-start | bytes 589832 | tf_op jit(solution)/shard_map/ppermute | solution.py:435
  3.0 13.7 %collective-permute-start.11 = (bf16[128,768]{1,0:T(8,128)(2,1)}, bf16[128,768]{1,0:T(8,128)(2,1)S(1)}, u32[]{:S(2)}, u32[]{:S(2)}) collective-permute-start(bf16[128,768]{1,0:T(8,128)(2,1)} %features_hbm.3), channel_id=1, source_target_pairs={{0,8},{8,0},{16,24},{24,16},{1,9},{9,1},{17,25},{25,17},{2,10},{10... | collective-permute-start | bytes 589832 | tf_op jit(solution)/shard_map/ppermute | solution.py:435
  4.5 12.7 %collective-permute-start.15 = (bf16[128,768]{1,0:T(8,128)(2,1)}, bf16[128,768]{1,0:T(8,128)(2,1)S(1)}, u32[]{:S(2)}, u32[]{:S(2)}) collective-permute-start(bf16[128,768]{1,0:T(8,128)(2,1)} %features_hbm.3), channel_id=1, source_target_pairs={{0,24},{8,16},{16,8},{24,0},{1,25},{9,17},{17,9},{25,1},{2,26},{10... | collective-permute-start | bytes 589832 | tf_op jit(solution)/shard_map/ppermute | solution.py:435
  5.6 5.7 %collective-permute-start.7 = (s32[8,128]{1,0:T(8,128)S(1)}, s32[8,128]{1,0:T(8,128)S(1)}, u32[]{:S(2)}, u32[]{:S(2)}) collective-permute-start(s32[8,128]{1,0:T(8,128)S(1)} %get-tuple-element.48.refs_1_), channel_id=1, source_target_pairs={{0,2},{1,3},{2,4},{3,5},{4,6},{5,7},{6,0},{7,1},{8,10},{9,11},{10,... | collective-permute-start | bytes 12296 | tf_op jit(solution)/shard_map/ppermute | solution.py:450
  7.7 6.3 %collective-permute-start.8 = (s32[8,128]{1,0:T(8,128)S(1)}, s32[8,128]{1,0:T(8,128)S(1)}, u32[]{:S(2)}, u32[]{:S(2)}) collective-permute-start(s32[8,128]{1,0:T(8,128)S(1)} %get-tuple-element.49.refs_2_), channel_id=1, source_target_pairs={{0,4},{1,5},{2,6},{3,7},{4,0},{5,1},{6,2},{7,3},{8,12},{9,13},{10,... | collective-permute-start | bytes 12296 | tf_op jit(solution)/shard_map/ppermute | solution.py:450
  11.3 3.6 %collective-permute-start = (s32[8,128]{1,0:T(8,128)S(1)}, s32[8,128]{1,0:T(8,128)S(1)}, u32[]{:S(2)}, u32[]{:S(2)}) collective-permute-start(s32[8,128]{1,0:T(8,128)S(1)} %get-tuple-element.52), channel_id=1, source_target_pairs={{0,8},{8,0},{16,24},{24,16},{1,9},{9,1},{17,25},{25,17},{2,10},{10... | collective-permute-start | bytes 12296 | tf_op jit(solution)/shard_map/ppermute | solution.py:473
  14.0 10.8 %collective-permute-start.10 = (bf16[128,768]{1,0:T(8,128)(2,1)}, bf16[128,768]{1,0:T(8,128)(2,1)S(1)}, u32[]{:S(2)}, u32[]{:S(2)}) collective-permute-start(bf16[128,768]{1,0:T(8,128)(2,1)} %features_hbm.3), channel_id=1, source_target_pairs={{0,1},{1,0},{2,3},{3,2},{4,5},{5,4},{6,7},{7,6},{8,9},{9,8},{10,11... | collective-permute-start | bytes 589832 | tf_op jit(solution)/shard_map/ppermute | solution.py:436
  14.9 3.6 %collective-permute-start.1 = (s32[8,128]{1,0:T(8,128)S(1)}, s32[8,128]{1,0:T(8,128)S(1)}, u32[]{:S(2)}, u32[]{:S(2)}) collective-permute-start(s32[8,128]{1,0:T(8,128)S(1)} %get-tuple-element.53), channel_id=1, source_target_pairs={{0,16},{8,24},{16,0},{24,8},{1,17},{9,25},{17,1},{25,9},{2,18},{10... | collective-permute-start | bytes 12296 | tf_op jit(solution)/shard_map/ppermute | solution.py:473
  16.7 8.1 %collective-permute-start.14 = (bf16[128,768]{1,0:T(8,128)(2,1)S(1)}, bf16[128,768]{1,0:T(8,128)(2,1)S(1)}, u32[]{:S(2)}, u32[]{:S(2)}) collective-permute-start(bf16[128,768]{1,0:T(8,128)(2,1)S(1)} %collective-permute-done.13.refs_8_), channel_id=1, source_target_pairs={{0,1},{1,0},{2,3},{3,2},{4,5},{5,4},{6,7},{7,6},{8,9},{9,8},{10,11... | collective-permute-start | bytes 589832 | tf_op jit(solution)/shard_map/ppermute | solution.py:436
  16.7 8.1 %collective-permute-start.12 = (bf16[128,768]{1,0:T(8,128)(2,1)S(1)}, bf16[128,768]{1,0:T(8,128)(2,1)S(1)}, u32[]{:S(2)}, u32[]{:S(2)}) collective-permute-start(bf16[128,768]{1,0:T(8,128)(2,1)S(1)} %collective-permute-done.11.refs_6_), channel_id=1, source_target_pairs={{0,1},{1,0},{2,3},{3,2},{4,5},{5,4},{6,7},{7,6},{8,9},{9,8},{10,11... | collective-permute-start | bytes 589832 | tf_op jit(solution)/shard_map/ppermute | solution.py:436
  17.2 7.6 %collective-permute-start.16 = (bf16[128,768]{1,0:T(8,128)(2,1)S(1)}, bf16[128,768]{1,0:T(8,128)(2,1)S(1)}, u32[]{:S(2)}, u32[]{:S(2)}) collective-permute-start(bf16[128,768]{1,0:T(8,128)(2,1)S(1)} %collective-permute-done.15.refs_10_), channel_id=1, source_target_pairs={{0,1},{1,0},{2,3},{3,2},{4,5},{5,4},{6,7},{7,6},{8,9},{9,8},{10,11... | collective-permute-start | bytes 589832 | tf_op jit(solution)/shard_map/ppermute | solution.py:436
  18.5 3.9 %collective-permute-start.9 = (s32[8,128]{1,0:T(8,128)S(1)}, s32[8,128]{1,0:T(8,128)S(1)}, u32[]{:S(2)}, u32[]{:S(2)}) collective-permute-start(s32[8,128]{1,0:T(8,128)S(1)} %get-tuple-element.50.refs_3_), channel_id=1, source_target_pairs={{0,6},{1,7},{2,0},{3,1},{4,2},{5,3},{6,4},{7,5},{8,14},{9,15},{10,... | collective-permute-start | bytes 12296 | tf_op jit(solution)/shard_map/ppermute | solution.py:450
  22.4 7.4 %collective-permute-start.2 = (s32[8,128]{1,0:T(8,128)S(1)}, s32[8,128]{1,0:T(8,128)S(1)}, u32[]{:S(2)}, u32[]{:S(2)}) collective-permute-start(s32[8,128]{1,0:T(8,128)S(1)} %get-tuple-element.54), channel_id=1, source_target_pairs={{0,24},{8,16},{16,8},{24,0},{1,25},{9,17},{17,9},{25,1},{2,26},{10... | collective-permute-start | bytes 12296 | tf_op jit(solution)/shard_map/ppermute | solution.py:473
  25.5 14.9 %collective-permute-start.17 = (bf16[48,768]{1,0:T(8,128)(2,1)S(1)}, bf16[48,768]{1,0:T(8,128)(2,1)S(1)}, u32[]{:S(2)}, u32[]{:S(2)}) collective-permute-start(bf16[48,768]{1,0:T(8,128)(2,1)S(1)} %get-tuple-element.61), channel_id=1, source_target_pairs={{0,6},{1,7},{2,0},{3,1},{4,2},{5,3},{6,4},{7,5},{8,14},{9,15},{10,... | collective-permute-start | bytes 221192 | tf_op jit(solution)/shard_map/ppermute | solution.py:483
  29.2 11.2 %collective-permute-start.18 = (bf16[48,768]{1,0:T(8,128)(2,1)S(1)}, bf16[48,768]{1,0:T(8,128)(2,1)S(1)}, u32[]{:S(2)}, u32[]{:S(2)}) collective-permute-start(bf16[48,768]{1,0:T(8,128)(2,1)S(1)} %get-tuple-element.62), channel_id=1, source_target_pairs={{0,4},{1,5},{2,6},{3,7},{4,0},{5,1},{6,2},{7,3},{8,12},{9,13},{10,... | collective-permute-start | bytes 221192 | tf_op jit(solution)/shard_map/ppermute | solution.py:483
  29.2 11.3 %collective-permute-start.19 = (bf16[48,768]{1,0:T(8,128)(2,1)S(1)}, bf16[48,768]{1,0:T(8,128)(2,1)S(1)}, u32[]{:S(2)}, u32[]{:S(2)}) collective-permute-start(bf16[48,768]{1,0:T(8,128)(2,1)S(1)} %get-tuple-element.63), channel_id=1, source_target_pairs={{0,2},{1,3},{2,4},{3,5},{4,6},{5,7},{6,0},{7,1},{8,10},{9,11},{10,... | collective-permute-start | bytes 221192 | tf_op jit(solution)/shard_map/ppermute | solution.py:483
  29.8 1.2 %collective-permute-start.3 = (s32[32,128]{1,0:T(8,128)S(1)}, s32[32,128]{1,0:T(8,128)S(1)}, u32[]{:S(2)}, u32[]{:S(2)}) collective-permute-start(s32[32,128]{1,0:T(8,128)S(1)} %constant_dynamic-update-slice_fusion.kept_ref), channel_id=1, source_target_pairs={{0,1},{1,0},{2,3},{3,2},{4,5},{5,4},{6,7},{7,6},{8,9},{9,8},{10,11... | collective-permute-start | bytes 49160 | tf_op jit(solution)/shard_map/ppermute | solution.py:474
  31.2 5.4 %collective-permute-start.4 = (s32[8,128]{1,0:T(8,128)S(1)}, s32[8,128]{1,0:T(8,128)S(1)}, u32[]{:S(2)}, u32[]{:S(2)}) collective-permute-start(s32[8,128]{1,0:T(8,128)S(1)} %get-tuple-element.56), channel_id=1, source_target_pairs={{0,2},{1,3},{2,4},{3,5},{4,6},{5,7},{6,0},{7,1},{8,10},{9,11},{10,... | collective-permute-start | bytes 12296 | tf_op jit(solution)/shard_map/ppermute | solution.py:492
  34.0 4.5 %collective-permute-start.5 = (s32[8,128]{1,0:T(8,128)S(1)}, s32[8,128]{1,0:T(8,128)S(1)}, u32[]{:S(2)}, u32[]{:S(2)}) collective-permute-start(s32[8,128]{1,0:T(8,128)S(1)} %get-tuple-element.57), channel_id=1, source_target_pairs={{0,4},{1,5},{2,6},{3,7},{4,0},{5,1},{6,2},{7,3},{8,12},{9,13},{10,... | collective-permute-start | bytes 12296 | tf_op jit(solution)/shard_map/ppermute | solution.py:492
  36.6 3.6 %collective-permute-start.6 = (s32[8,128]{1,0:T(8,128)S(1)}, s32[8,128]{1,0:T(8,128)S(1)}, u32[]{:S(2)}, u32[]{:S(2)}) collective-permute-start(s32[8,128]{1,0:T(8,128)S(1)} %get-tuple-element.58), channel_id=1, source_target_pairs={{0,6},{1,7},{2,0},{3,1},{4,2},{5,3},{6,4},{7,5},{8,14},{9,15},{10,... | collective-permute-start | bytes 12296 | tf_op jit(solution)/shard_map/ppermute | solution.py:492
  42.3 15.3 %all-to-all-start = ((bf16[32,3,2,768]{3,2,1,0:T(2,128)(2,1)}), bf16[32,3,2,768]{3,2,1,0:T(2,128)(2,1)S(1)}, u32[]{:S(2)}, u32[]{:S(2)}) async-start(bf16[32,3,2,768]{3,2,1,0:T(2,128)(2,1)} %get-tuple-element.71), calls=%async_computation | async-start | bytes 589824 | tf_op jit(solution)/shard_map/all_to_all | solution.py:509
  57.6 10.9 %copy-start = (bf16[128,128]{1,0:T(8,128)(2,1)S(1)}, bf16[128,128]{1,0:T(8,128)(2,1)}, u32[]{:S(2)}) copy-start(bf16[128,128]{1,0:T(8,128)(2,1)} %get-tuple-element.66.place_ref) | copy-start | bytes 98308
  59.8 6.9 %collective-permute-start.20 = (bf16[32,1024]{1,0:T(8,128)(2,1)S(1)}, bf16[32,1024]{1,0:T(8,128)(2,1)S(1)}, u32[]{:S(2)}, u32[]{:S(2)}) collective-permute-start(bf16[32,1024]{1,0:T(8,128)(2,1)S(1)} %get-tuple-element.74), channel_id=1, source_target_pairs={{0,2},{1,3},{2,4},{3,5},{4,6},{5,7},{6,0},{7,1},{8,10},{9,11},{10,... | collective-permute-start | bytes 196616 | tf_op jit(solution)/shard_map/ppermute | solution.py:549
  59.9 8.6 %collective-permute-start.21 = (bf16[32,1024]{1,0:T(8,128)(2,1)S(1)}, bf16[32,1024]{1,0:T(8,128)(2,1)S(1)}, u32[]{:S(2)}, u32[]{:S(2)}) collective-permute-start(bf16[32,1024]{1,0:T(8,128)(2,1)S(1)} %get-tuple-element.75), channel_id=1, source_target_pairs={{0,4},{1,5},{2,6},{3,7},{4,0},{5,1},{6,2},{7,3},{8,12},{9,13},{10,... | collective-permute-start | bytes 196616 | tf_op jit(solution)/shard_map/ppermute | solution.py:549
  60.3 8.2 %collective-permute-start.22 = (bf16[32,1024]{1,0:T(8,128)(2,1)S(1)}, bf16[32,1024]{1,0:T(8,128)(2,1)S(1)}, u32[]{:S(2)}, u32[]{:S(2)}) collective-permute-start(bf16[32,1024]{1,0:T(8,128)(2,1)S(1)} %get-tuple-element.76), channel_id=1, source_target_pairs={{0,6},{1,7},{2,0},{3,1},{4,2},{5,3},{6,4},{7,5},{8,14},{9,15},{10,... | collective-permute-start | bytes 196616 | tf_op jit(solution)/shard_map/ppermute | solution.py:549
